TPU v7x, 32 devices: a whole 2x2x4 slice. The times are simulated.
32 devices in a mesh: grp: 2 (over y), pair: 4 (over z), aux: 2 (over x), rep: 2 (over core).
Axes of the slice: x: 2, y: 2, z: 4, core: 2. Of those that a mesh axis runs over, the one named last changes fastest.
Arguments:
- three_center: bfloat16 [5120, 4, 8000], P(('grp', 'aux', 'rep', 'pair')), parts along dimension 0, may hold values from -0.050591038 to 0.050591038
- eps_occ: float32 [8], P('grp'), parts along dimension 0, may hold values from -1.2 to -0.4
- eps_virt: float32 [16000], P(('grp', 'pair')), parts along dimension 0, may hold values from 0.2 to 3
- freq: float32 [2], P('grp'), parts along dimension 0, may hold values from 0.2 to 2
Outputs:
- polar: float32 [5120, 2560], P(('grp', 'aux', 'rep'), 'pair'), parts along dimension 0
There are 2 independent parts, one for each index of `grp`. A program takes and returns all parts, laid end to end along the dimension named above; each array names one. Nothing has to cross between parts.
All inputs are finite; a program needn't handle non-finite values.
Results may differ from a plain program's by a relative error of at most 0.0003.
Values may be sent and summed in bfloat16 or wider, within the bound.
A program may use at most 192 MiB of HBM per device.

v0:
```python
import jax
import jax.numpy as jnp
from jax import lax
from jax.sharding import PartitionSpec as P


def local(three_center, eps_occ, eps_virt, freq):
    arrived = lax.all_to_all(three_center, "pair", split_axis=2, concat_axis=0, tiled=True)
    excite = eps_virt[None, :] - eps_occ[:, None]
    weight = 2.0 * excite / (excite * excite + freq[0] * freq[0])
    height = arrived.shape[0]
    scaled = (
        (arrived.astype(jnp.float32) * weight[None, :, :]).astype(jnp.bfloat16).reshape(height, -1)
    )
    plain_rows = arrived.reshape(height, -1)
    partial_sums = lax.dot_general(
        scaled,
        lax.all_gather(plain_rows, ("aux", "rep"), axis=0, tiled=True),
        (((1,), (1,)), ((), ())),
        preferred_element_type=jnp.float32,
    )
    return lax.psum_scatter(partial_sums, "pair", scatter_dimension=1, tiled=True)


def solution(mesh):
    return jax.shard_map(
        local,
        mesh=mesh,
        in_specs=(
            P(("grp", "aux", "rep", "pair"), None, None),
            P("grp"),
            P(("grp", "pair")),
            P("grp"),
        ),
        out_specs=P(("grp", "aux", "rep"), "pair"),
        check_vma=False,
    )
```

profile of v0, /device:TPU:0, one launch (start us, length us, event | category | flops | bytes accessed | tf_op | source)
XLA Modules:
  0.0 865.8 jit_solution(16826013014737475002)
XLA Ops:
  6.5 0.0 copy-start
  6.5 0.0 all-gather.2.cloned.1.call-start
  6.5 32.8 %copy.8 = bf16[160,4,8000]{0,1,2:T(4,128)(2,1)} copy(bf16[160,4,8000]{2,1,0:T(4,128)(2,1)} %param.4) | data formatting | bytes 20480000 | tf_op args[0]
  39.3 367.0 %all_to_all.18 = bf16[160,4,8000]{0,1,2:T(4,128)(2,1)} all-to-all(bf16[160,4,8000]{0,1,2:T(4,128)(2,1)} %copy.8), channel_id=1, replica_groups=mesh['grp'=2,'pair'=4,'aux'=2,'rep'=2] {'pair'}, dimensions={2} | all-to-all | bytes 20480000 | tf_op jit(solution)/shard_map/all_to_all | solution.py:8
  406.3 35.7 %copy.9 = bf16[160,4,4,2000]{3,1,0,2:T(4,128)(2,1)} copy(bf16[160,4,4,2000]{0,1,3,2:T(4,128)(2,1)} %bitcast.4) | data formatting | bytes 20480000 | tf_op jit(solution)/shard_map/all_to_all | solution.py:8
  442.0 0.0 copy-start.2
  442.0 20.3 %all_to_all.16 = bf16[640,8000]{1,0:T(8,128)(2,1)} reshape(bf16[4,160,4,2000]{3,2,1,0:T(4,128)(2,1)} %bitcast.5) | data formatting | bytes 20480000 | tf_op jit(solution)/shard_map/all_to_all | solution.py:8
  462.3 0.0 all-gather.2.cloned.1.call-update
  462.3 0.0 reduce-scatter.2.cloned.1.call-start
  463.0 0.0 copy-done
  463.1 0.1 broadcast_reduce_fusion
  463.2 0.1 sub.24
  463.3 0.0 copy-done.2
  463.3 0.1 sub.22
  463.4 245.1 %all-gather.2.cloned.1.call-done = bf16[2560,8000]{1,0:T(8,128)(2,1)} async-done(((bf16[640,8000]{1,0:T(8,128)(2,1)}), bf16[2560,8000]{1,0:T(8,128)(2,1)}) %all-gather.2.cloned.1.call-update) | async-done | bytes 40960016 | tf_op jit(solution)/shard_map/all_gather | solution.py:18
  708.5 0.0 copy-start.1
  708.5 35.3 %fusion = f32[640,2560]{1,0:T(8,128)} fusion(bf16[2560,8000]{1,0:T(8,128)(2,1)} %all-gather.2.cloned.1.call-done, bf16[640,8000]{1,0:T(8,128)(2,1)} %all_to_all.16, f32[8000]{0:T(1024)S(1)} %add_divide_fusion), kind=kOutput, calls=%fused_computation.1 | convolution fusion | flops 26229760000 | bytes 57785600 | tf_op jit(solution)/shard_map/dot_general | solution.py:16
  743.8 0.0 reduce-scatter.2.cloned.1.call-update
  743.8 115.2 %reduce-scatter.2.cloned.1.call-done = f32[640,640]{1,0:T(8,128)} async-done(((f32[640,2560]{1,0:T(8,128)}), f32[640,640]{1,0:T(8,128)}) %reduce-scatter.2.cloned.1.call-update) | async-done | bytes 1638416 | tf_op jit(solution)/shard_map/reduce_scatter | solution.py:22
  859.0 0.0 copy-done.1
  (2 shorter events, 0.0 us)
Async XLA Ops:
  6.5 456.5 %copy-start = (f32[4]{0:T(128)S(1)}, f32[4]{0:T(128)}, u32[]{:S(2)}) copy-start(f32[4]{0:T(128)} %param.5) | copy-start | bytes 52
  6.5 701.9 %all-gather.2.cloned.1.call-start = ((), (), s32[]{:S(2)}) async-start(), calls=%async_computation.2 | async-start | bytes 51609600 | tf_op jit(solution)/shard_map/all_gather | solution.py:18
  442.0 21.3 %copy-start.2 = (f32[2000]{0:T(1024)S(1)}, f32[2000]{0:T(1024)}, u32[]{:S(2)}) copy-start(f32[2000]{0:T(1024)} %param.6) | copy-start | bytes 24004
  462.3 396.6 %reduce-scatter.2.cloned.1.call-start = ((), (), s32[]{:S(2)}) async-start(), calls=%async_computation.3 | async-start | bytes 8192000 | tf_op jit(solution)/shard_map/reduce_scatter | solution.py:22
  708.5 150.5 %copy-start.1 = (f32[4]{0:T(128)S(1)}, f32[4]{0:T(128)}, u32[]{:S(2)}) copy-start(f32[4]{0:T(128)} %param.5) | copy-start | bytes 52
Sparse Core Ops, SparseCore 0:
  462.5 245.9 all-gather.1
  744.0 115.0 reduce-scatter.1
where the time goes:
time: 869 us; the launch traced here: 866 us
  blocking collectives  367 us (42%)
  waiting for transfers between devices  360 us (41%)
  local copies, waits for them, and re-layouts  89.1 us (10%)
  matrix products  35.3 us (4%)
  between operations  14.1 us (2%)
    all_to_all x1, blocking collectives, local(): lax.all_to_all(three_center, 'pair', split_axis=2, concat_axis=0, tiled=T...  367 us
    all_gather x1, waiting for transfers between devices, local(): lax.all_gather(plain_rows, ('aux', 'rep'), axis=0, tiled=True)  245 us
    reduce_scatter x1, waiting for transfers between devices, local(): lax.psum_scatter(partial_sums, 'pair', scatter_dimension=1, tiled=True)  115 us
    all_to_all x2, local copies, waits for them, and re-layouts, local(): lax.all_to_all(three_center, 'pair', split_axis=2, concat_axis=0, tiled=T...  56 us
    dot_general x1, matrix products, local(): lax.dot_general(scaled, lax.all_gather(plain_rows, ('aux', 'rep'), axis=0...  35.3 us
    unnamed x7, local copies, waits for them, and re-layouts  32.8 us
  transfers between devices with their start and end apart: 2, of which 2 were waited for; matrix products, arithmetic and copies ran while one was open for 0% of the time, Pallas kernels for 0%

commit v1 on v0

--- a/solution.py
+++ b/solution.py
@@ -4,8 +4,37 @@
 from jax.sharding import PartitionSpec as P
 
 
+def reach_things_on_mesh(field, where_dim, inp):
+    vec_out, piece_next = (field.shape[:where_dim], field.shape[where_dim + 1 :])
+    odd = field.reshape(*vec_out, inp, -1, *piece_next)
+    work_now = jnp.moveaxis(odd, where_dim, 0)
+    return work_now
+
+
+def load_the_roots(sheet, dimension_no):
+    sheet = jnp.moveaxis(sheet, 0, dimension_no)
+    a_now = sheet.shape
+    taken_in = sheet.reshape(
+        *a_now[:dimension_no],
+        a_now[dimension_no] * a_now[dimension_no + 1],
+        *a_now[dimension_no + 2 :]
+    )
+    return taken_in
+
+
 def local(three_center, eps_occ, eps_virt, freq):
-    arrived = lax.all_to_all(three_center, "pair", split_axis=2, concat_axis=0, tiled=True)
+    mid_arr = lax.axis_index("pair")
+    e_now = lax.axis_size("pair")
+    all_rows, met_up = (e_now, mid_arr)
+    carry = reach_things_on_mesh(three_center, 2, all_rows)
+    panels = [carry[met_up]]
+    for dd in range(1, all_rows):
+        outer = carry[met_up ^ dd]
+        arr_now = lax.ppermute(outer, "pair", [(h, h ^ dd) for h in range(all_rows)])
+        panels.append(arr_now)
+    next_value = jnp.stack(panels)
+    carry = next_value[met_up ^ jnp.arange(all_rows)]
+    arrived = load_the_roots(carry, 0)
     excite = eps_virt[None, :] - eps_occ[:, None]
     weight = 2.0 * excite / (excite * excite + freq[0] * freq[0])
     height = arrived.shape[0]

time: 869 us -> 772 us (0.89)
  blocking collectives: 367 us -> 0 us
  waiting for transfers between devices: 360 us -> 576 us
  local copies, waits for them, and re-layouts: 89.1 us -> 131 us
    all_to_all x1 -> x0, blocking collectives: 367 us -> none  [local(): lax.all_to_all(three_center, 'pair', split_axis=2, concat_axis=0, tiled=T...]
    ppermute x0 -> x3, waiting for transfers between devices: none -> 215 us  [local(): lax.ppermute(outer, 'pair', [(h, h ^ dd) for h in range(all_rows)])]
    all_to_all x2 -> x0, local copies, waits for them, and re-layouts: 56 us -> none  [local(): lax.all_to_all(three_center, 'pair', split_axis=2, concat_axis=0, tiled=T...]
    reshape x0 -> x2, local copies, waits for them, and re-layouts: none -> 44.6 us  [the longest x1 24.2 us: reach_things_on_mesh(): odd = field.reshape(*vec_out, inp, -1, *piece_next)]
    another operation x0 -> x1, local copies, waits for them, and re-layouts: none -> 33.1 us
    gather x0 -> x4, local copies, waits for them, and re-layouts: none -> 17.8 us  [local(): carry = next_value[met_up ^ jnp.arange(all_rows)]]
    unnamed x7 -> x11, local copies, waits for them, and re-layouts: 32.8 us -> 35.4 us
  transfers between devices with their start and end apart: 2 -> 5, of which waited for: 2 -> 5; matrix products, arithmetic and copies ran while one was open for 0% -> 1% of each run, Pallas kernels for 0% -> 0%
where the time goes in v1:
time: 772 us; the launch traced here: 771 us
  waiting for transfers between devices  576 us (75%)
  local copies, waits for them, and re-layouts  131 us (17%)
  matrix products  35.5 us (5%)
  between operations  14.2 us (2%)
    all_gather x1, waiting for transfers between devices, local(): lax.all_gather(plain_rows, ('aux', 'rep'), axis=0, tiled=True)  246 us
    ppermute x3, waiting for transfers between devices, local(): lax.ppermute(outer, 'pair', [(h, h ^ dd) for h in range(all_rows)])  215 us
    reduce_scatter x1, waiting for transfers between devices, local(): lax.psum_scatter(partial_sums, 'pair', scatter_dimension=1, tiled=True)  115 us
    dot_general x1, matrix products, local(): lax.dot_general(scaled, lax.all_gather(plain_rows, ('aux', 'rep'), axis=0...  35.5 us
    unnamed x11, local copies, waits for them, and re-layouts  35.4 us
    another operation x1, local copies, waits for them, and re-layouts  33.1 us
    reshape x1, local copies, waits for them, and re-layouts, reach_things_on_mesh(): odd = field.reshape(*vec_out, inp, -1, *piece_next)  24.2 us
    reshape x1, local copies, waits for them, and re-layouts, load_the_roots(): sheet.reshape(*a_now[:dimension_no], a_now[dimension_no] * a_now[dimensio...  20.3 us
  transfers between devices with their start and end apart: 5, of which 5 were waited for; matrix products, arithmetic and copies ran while one was open for 1% of the time, Pallas kernels for 0%

profile of v1, /device:TPU:0, one launch (start us, length us, event | category | flops | bytes accessed | tf_op | source)
XLA Modules:
  0.0 770.5 jit_solution(17815522248175711828)
XLA Ops:
  6.5 0.0 copy-start
  6.5 0.0 all-gather.2.cloned.1.call-start
  6.5 24.2 %reshape.79 = bf16[160,4,4,2000]{3,2,1,0:T(4,128)(2,1)} reshape(bf16[160,4,8000]{2,1,0:T(4,128)(2,1)} %param.4) | data formatting | bytes 20480000 | tf_op jit(solution)/shard_map/reshape | solution.py:9
  30.8 33.1 %constant_dynamic-slice_fusion.3 = (bf16[160,4,1,2000]{3,2,1,0:T(2,128)(2,1)S(1)}, bf16[160,4,1,2000]{3,2,1,0:T(2,128)(2,1)S(1)}, bf16[160,4,1,2000]{3,2,1,0:T(2,128)(2,1)S(1)}, bf16[160,4,1,2000]{3,2,1,0:T(2,128)(2,1)S(1)}) fusion(bf16[160,4,4,2000]{3,2,1,0:T(4,128)(2,1)} %reshape.79, s32[]{:T(128)S(6)} %select_n.22, s32[]{:T(128)S(6)} %select_n.24, ...), kind=kLoop, calls=%fused_computation.18 | loop fusion | bytes 20480016 | tf_op jit(solution)/shard_map/dynamic-slice
  63.9 2.8 copy.33
  66.7 5.1 collective-permute-start.2
  71.8 2.8 copy.35
  74.6 0.1 collective-permute-start
  74.7 2.8 copy.34
  77.5 0.6 collective-permute-start.1
  78.1 2.8 copy.36
  80.9 0.2 pad_clamp_fusion
  81.2 48.4 %collective-permute-done.2 = bf16[160,4,2000]{2,0,1:T(8,128)(2,1)S(1)} collective-permute-done((bf16[160,4,2000]{2,0,1:T(8,128)(2,1)S(1)}, bf16[160,4,2000]{2,0,1:T(8,128)(2,1)S(1)}, u32[]{:S(2)}, u32[]{:S(2)}) %collective-permute-start.2) | collective-permute-done | bytes 2560032 | tf_op jit(solution)/shard_map/ppermute | solution.py:33
  129.6 56.4 %collective-permute-done = bf16[160,4,2000]{2,0,1:T(8,128)(2,1)S(1)} collective-permute-done((bf16[160,4,2000]{2,0,1:T(8,128)(2,1)S(1)}, bf16[160,4,2000]{2,0,1:T(8,128)(2,1)S(1)}, u32[]{:S(2)}, u32[]{:S(2)}) %collective-permute-start) | collective-permute-done | bytes 2560032 | tf_op jit(solution)/shard_map/ppermute | solution.py:33
  186.0 110.4 %collective-permute-done.1 = bf16[160,4,2000]{2,0,1:T(8,128)(2,1)S(1)} collective-permute-done((bf16[160,4,2000]{2,0,1:T(8,128)(2,1)S(1)}, bf16[160,4,2000]{2,0,1:T(8,128)(2,1)S(1)}, u32[]{:S(2)}, u32[]{:S(2)}) %collective-permute-start.1) | collective-permute-done | bytes 2560032 | tf_op jit(solution)/shard_map/ppermute | solution.py:33
  296.4 1.4 pad_maximum_fusion
  297.8 3.2 mini-gather-slice.2
  301.0 3.2 mini-gather-slice.3
  304.2 5.7 gather_fusion.1
  309.9 5.7 gather_fusion
  315.6 5.7 pad_maximum_fusion.1
  321.3 24.2 %copy.7 = bf16[4,160,4,2000]{3,2,1,0:T(4,128)(2,1)} copy(bf16[4,160,4,2000]{3,1,2,0:T(8,128)(2,1)S(1)} %pad_maximum_fusion.1) | data formatting | bytes 20480000
  345.5 20.3 %reshape.62 = bf16[640,8000]{1,0:T(8,128)(2,1)} reshape(bf16[4,160,4,2000]{3,2,1,0:T(4,128)(2,1)} %copy.7) | data formatting | bytes 20480000 | tf_op jit(solution)/shard_map/reshape | solution.py:17
  365.9 0.0 copy-start.2
  365.9 0.0 all-gather.2.cloned.1.call-update
  365.9 0.0 reduce-scatter.2.cloned.1.call-start
  366.6 0.0 copy-done
  366.6 0.1 broadcast_reduce_fusion
  366.7 0.1 sub.24
  366.8 0.0 copy-done.2
  366.8 0.1 sub.22
  366.9 246.1 %all-gather.2.cloned.1.call-done = bf16[2560,8000]{1,0:T(8,128)(2,1)} async-done(((bf16[640,8000]{1,0:T(8,128)(2,1)}), bf16[2560,8000]{1,0:T(8,128)(2,1)}) %all-gather.2.cloned.1.call-update) | async-done | bytes 40960016 | tf_op jit(solution)/shard_map/all_gather | solution.py:47
  613.0 0.0 copy-start.1
  613.0 35.5 %fusion = f32[640,2560]{1,0:T(8,128)} fusion(bf16[2560,8000]{1,0:T(8,128)(2,1)} %all-gather.2.cloned.1.call-done, bf16[640,8000]{1,0:T(8,128)(2,1)} %reshape.62, f32[8000]{0:T(1024)S(1)} %add_divide_fusion), kind=kOutput, calls=%fused_computation.5 | convolution fusion | flops 26229760000 | bytes 57785600 | tf_op jit(solution)/shard_map/dot_general | solution.py:45
  648.5 0.0 reduce-scatter.2.cloned.1.call-update
  648.5 115.2 %reduce-scatter.2.cloned.1.call-done = f32[640,640]{1,0:T(8,128)} async-done(((f32[640,2560]{1,0:T(8,128)}), f32[640,640]{1,0:T(8,128)}) %reduce-scatter.2.cloned.1.call-update) | async-done | bytes 1638416 | tf_op jit(solution)/shard_map/reduce_scatter | solution.py:51
  763.7 0.0 copy-done.1
  (3 shorter events, 0.0 us)
Async XLA Ops:
  6.5 360.1 %copy-start = (f32[4]{0:T(128)S(1)}, f32[4]{0:T(128)}, u32[]{:S(2)}) copy-start(f32[4]{0:T(128)} %param.5) | copy-start | bytes 52
  6.5 606.5 %all-gather.2.cloned.1.call-start = ((), (), s32[]{:S(2)}) async-start(), calls=%async_computation.1 | async-start | bytes 51609600 | tf_op jit(solution)/shard_map/all_gather | solution.py:47
  66.7 62.9 %collective-permute-start.2 = (bf16[160,4,2000]{2,0,1:T(8,128)(2,1)S(1)}, bf16[160,4,2000]{2,0,1:T(8,128)(2,1)S(1)}, u32[]{:S(2)}, u32[]{:S(2)}) collective-permute-start(bf16[160,4,2000]{2,0,1:T(8,128)(2,1)S(1)} %bitcast.27), channel_id=1, source_target_pairs={{0,12},{4,8},{8,4},{12,0},{1,13},{5,9},{9,5},{13,1},{2,14},{6,10},... | collective-permute-start | bytes 7680008 | tf_op jit(solution)/shard_map/ppermute | solution.py:33
  74.6 111.4 %collective-permute-start = (bf16[160,4,2000]{2,0,1:T(8,128)(2,1)S(1)}, bf16[160,4,2000]{2,0,1:T(8,128)(2,1)S(1)}, u32[]{:S(2)}, u32[]{:S(2)}) collective-permute-start(bf16[160,4,2000]{2,0,1:T(8,128)(2,1)S(1)} %bitcast.28), channel_id=1, source_target_pairs={{0,4},{4,0},{8,12},{12,8},{1,5},{5,1},{9,13},{13,9},{2,6},{6,2},{1... | collective-permute-start | bytes 7680008 | tf_op jit(solution)/shard_map/ppermute | solution.py:33
  77.5 218.9 %collective-permute-start.1 = (bf16[160,4,2000]{2,0,1:T(8,128)(2,1)S(1)}, bf16[160,4,2000]{2,0,1:T(8,128)(2,1)S(1)}, u32[]{:S(2)}, u32[]{:S(2)}) collective-permute-start(bf16[160,4,2000]{2,0,1:T(8,128)(2,1)S(1)} %bitcast.29), channel_id=1, source_target_pairs={{0,8},{4,12},{8,0},{12,4},{1,9},{5,13},{9,1},{13,5},{2,10},{6,14},... | collective-permute-start | bytes 7680008 | tf_op jit(solution)/shard_map/ppermute | solution.py:33
  365.9 0.9 copy-start.2
  365.9 397.8 %reduce-scatter.2.cloned.1.call-start = ((), (), s32[]{:S(2)}) async-start(), calls=%async_computation.2 | async-start | bytes 8192000 | tf_op jit(solution)/shard_map/reduce_scatter | solution.py:51
  613.0 150.7 %copy-start.1 = (f32[4]{0:T(128)S(1)}, f32[4]{0:T(128)}, u32[]{:S(2)}) copy-start(f32[4]{0:T(128)} %param.5) | copy-start | bytes 52
Sparse Core Ops, SparseCore 0:
  366.0 246.9 all-gather.1
  648.6 115.0 reduce-scatter.1
